TPU v7x, 256 devices: a whole 4x4x8 slice. The times are simulated.
256 devices in a mesh: lat: 32 (over x, z), lead: 8 (over y, core).
Axes of the slice: x: 4, y: 4, z: 8, core: 2. Of those that a mesh axis runs over, the one named last changes fastest.
Arguments:
- latent: bfloat16 [32, 256, 64, 256], P('lat', None, 'lead'), may hold values from -6 to 6
- conv_weight: bfloat16 [3, 3, 256, 256], replicated, may hold values from -0.125 to 0.125
- conv_bias: float32 [256], replicated, may hold values from -4 to 4
- norm_gain: float32 [256], replicated, may hold values from 0.1 to 1.9
- w_query: bfloat16 [256, 256], replicated, may hold values from -12 to 12
- w_key: bfloat16 [256, 256], replicated, may hold values from -0.25 to 0.25
- w_value: bfloat16 [256, 256], replicated, may hold values from -0.375 to 0.375
- w_out: bfloat16 [256, 256], replicated, may hold values from -0.375 to 0.375
Outputs:
- section_out: bfloat16 [32, 256, 64, 256], P('lat', None, 'lead')
All inputs are finite; a program needn't handle non-finite values.
Results may differ from a plain program's by a relative error of at most 0.014.
Values may be sent and summed in bfloat16 or wider, within the bound.
No kernel may reach another device: no remote copies, remote signals or barrier semaphores. Data moves between devices by JAX's collectives and lax.ppermute only.
A program may use at most 128 MiB of HBM per device.

v0:
```python
import math
import jax
import jax.numpy as jnp
from jax import lax
from jax.sharding import PartitionSpec as P

HD = 32


def padded_2(block, sides, width):
    for axis, dim in sides:
        count = lax.axis_size(axis)
        forward = [(i, i + 1) for i in range(count - 1)]
        backward = [(target, source) for source, target in forward]
        low = lax.ppermute(
            lax.slice_in_dim(block, block.shape[dim] - width, None, axis=dim), axis, forward
        )
        high = lax.ppermute(lax.slice_in_dim(block, 0, width, axis=dim), axis, backward)
        block = jnp.concatenate([low, block, high], axis=dim)
    return block


def attend(query, keys, values):
    chans = query.shape[-1]
    heads = chans // HD
    q_shape = query.shape
    query = query.reshape(-1, q_shape[-2], heads, HD)
    keys = keys.reshape(-1, keys.shape[-2], heads, HD)
    values = values.reshape(-1, values.shape[-2], heads, HD)
    scores = jnp.einsum(
        "pqhd,pkhd->phqk", query, keys, preferred_element_type=jnp.float32
    ) / math.sqrt(HD)
    top = jnp.max(scores, axis=-1, keepdims=True)
    expo = jnp.exp(scores - top)
    weights = (expo / jnp.sum(expo, axis=-1, keepdims=True)).astype(jnp.bfloat16)
    attended = jnp.einsum("phqk,pkhd->pqhd", weights, values, preferred_element_type=jnp.float32)
    return attended.astype(jnp.bfloat16).reshape(q_shape)


def project(normed, weight):
    shape = normed.shape
    flat = jnp.dot(normed.reshape(-1, shape[-1]), weight, preferred_element_type=jnp.float32)
    return flat.astype(jnp.bfloat16).reshape(shape)


def shards(latent, conv_weight, conv_bias, norm_gain, w_query, w_key, w_value, w_out):
    nrows, width, leads, chans = latent.shape
    extended = padded_2(latent, (("lat", 0),), 1)
    padded = jnp.pad(extended, ((0, 0), (1, 1), (0, 0), (0, 0)))
    acc = jnp.zeros((nrows * width * leads, chans), jnp.float32)
    for a in range(3):
        for b in range(3):
            piece = padded[a : a + nrows, b : b + width].reshape(-1, chans)
            acc = acc + jnp.dot(piece, conv_weight[a, b], preferred_element_type=jnp.float32)
    hidden = jax.nn.gelu(acc + conv_bias, approximate=True).astype(jnp.bfloat16)
    hidden_f = hidden.astype(jnp.float32)
    mean = jnp.mean(hidden_f, axis=-1, keepdims=True)
    var = jnp.mean((hidden_f - mean) ** 2, axis=-1, keepdims=True)
    normed = ((hidden_f - mean) * lax.rsqrt(var + 1e-05) * norm_gain).astype(jnp.bfloat16)
    normed = normed.reshape(nrows, width, leads, chans)
    block = lax.all_to_all(normed, "lead", split_axis=1, concat_axis=2, tiled=True)
    attended_px = attend(project(block, w_query), project(block, w_key), project(block, w_value))
    attended = lax.all_to_all(attended_px, "lead", split_axis=2, concat_axis=1, tiled=True)
    mixed = hidden_f + jnp.dot(
        attended.reshape(-1, chans), w_out, preferred_element_type=jnp.float32
    )
    return mixed.astype(jnp.bfloat16).reshape(nrows, width, leads, chans)


def solution(mesh):
    in_specs = (P("lat", None, "lead", None), P(), P(), P(), P(), P(), P(), P())
    out_specs = P("lat", None, "lead", None)
    return jax.shard_map(shards, mesh=mesh, in_specs=in_specs, out_specs=out_specs, check_vma=False)
```

profile of v0, /device:TPU:6, one launch (start us, length us, event | category | flops | bytes accessed | tf_op | source)
XLA Modules:
  0.0 127.0 jit_solution(6796232368115607537)
XLA Ops:
  0.0 0.0 copy-start
  0.0 8.1 %collective-permute-start.1 = (bf16[1,256,8,256]{3,2,1,0:T(8,128)(2,1)}, bf16[1,256,8,256]{3,2,1,0:T(8,128)(2,1)S(1)}, u32[]{:S(2)}, u32[]{:S(2)}) collective-permute-start(bf16[1,256,8,256]{3,2,1,0:T(8,128)(2,1)} %param.8), channel_id=1, source_target_pairs={{8,0},{16,8},{24,16},{32,24},{40,32},{48,40},{56,48},{64,56},{72,6... | collective-permute-start | bytes 3145736 | tf_op jit(solution)/shard_map/ppermute | solution.py:18
  8.2 1.9 %collective-permute-start = (bf16[1,256,8,256]{3,2,1,0:T(8,128)(2,1)}, bf16[1,256,8,256]{3,2,1,0:T(8,128)(2,1)S(1)}, u32[]{:S(2)}, u32[]{:S(2)}) collective-permute-start(bf16[1,256,8,256]{3,2,1,0:T(8,128)(2,1)} %param.8), channel_id=1, source_target_pairs={{0,8},{8,16},{16,24},{24,32},{32,40},{40,48},{48,56},{56,64},{64,7... | collective-permute-start | bytes 3145736 | tf_op jit(solution)/shard_map/ppermute | solution.py:15
  10.1 1.7 %fusion.46 = f32[2048,256]{1,0:T(8,128)S(1)} fusion(bf16[1,256,8,256]{3,2,1,0:T(8,128)(2,1)} %param.8, bf16[3,3,256,256]{3,2,1,0:T(8,128)(2,1)} %param.9), kind=kOutput, calls=%fused_computation.61 | convolution fusion | flops 268435456 | bytes 3276800 | tf_op jit(solution)/shard_map/dot_general | solution.py:54
  11.8 0.0 copy-start.4
  11.8 19.1 %collective-permute-done.1 = bf16[1,256,8,256]{3,2,1,0:T(8,128)(2,1)S(1)} collective-permute-done((bf16[1,256,8,256]{3,2,1,0:T(8,128)(2,1)}, bf16[1,256,8,256]{3,2,1,0:T(8,128)(2,1)S(1)}, u32[]{:S(2)}, u32[]{:S(2)}) %collective-permute-start.1) | collective-permute-done | bytes 1048608 | tf_op jit(solution)/shard_map/ppermute | solution.py:18
  30.9 6.1 %collective-permute-done = bf16[1,256,8,256]{3,2,1,0:T(8,128)(2,1)S(1)} collective-permute-done((bf16[1,256,8,256]{3,2,1,0:T(8,128)(2,1)}, bf16[1,256,8,256]{3,2,1,0:T(8,128)(2,1)S(1)}, u32[]{:S(2)}, u32[]{:S(2)}) %collective-permute-start) | collective-permute-done | bytes 1048608 | tf_op jit(solution)/shard_map/ppermute | solution.py:15
  37.0 0.0 copy-done.2
  37.0 0.6 fusion.11
  37.6 0.0 copy-done.4
  37.6 0.4 fusion.40
  38.0 0.4 fusion.41
  38.4 0.4 fusion.42
  38.9 0.4 fusion.43
  39.3 0.4 fusion.39
  39.8 0.4 fusion.48
  40.2 0.0 copy-start.8
  40.2 0.4 fusion.44
  40.6 0.2 copy-done.8
  40.9 1.7 %convert_reduce_fusion = (f32[2048]{0:T(1024)S(1)}, bf16[2048,256]{1,0:T(8,128)(2,1)S(1)}) fusion(f32[256]{0:T(256)S(1)} %copy-done.8, f32[2048,256]{1,0:T(8,128)S(1)} %fusion.39, f32[2048,256]{1,0:T(8,128)S(1)} %fusion.44, f32[2048,256]{1,0:T(8,128)S(1)} %fusion.40, bf16[3,3,256,256]{3,2,1,0:T(8,128)(2,1)S(1)} %copy-done.4, ...), kind=kOutput, calls=%fused_computation.17 | convolution fusion | flops 278919168 | bytes 19014656 | tf_op jit(solution)/shard_map/dot_general | solution.py:54
  42.6 0.6 fusion.19
  43.3 0.0 copy-done.9
  43.3 0.7 fusion.38
  44.0 20.4 %all_to_all.30 = bf16[1,256,8,256]{3,2,0,1:T(8,128)(2,1)S(1)} all-to-all(bf16[1,256,8,256]{3,2,0,1:T(8,128)(2,1)S(1)} %fusion.38), channel_id=1, replica_groups=mesh['lat'=32,'lead'=8] {'lead'}, dimensions={1} | all-to-all | bytes 2097152 | tf_op jit(solution)/shard_map/all_to_all | solution.py:61
  64.4 0.1 copy.33
  64.5 0.0 copy-done
  64.6 1.4 %convolution_convert_fusion = bf16[2048,256]{1,0:T(8,128)(2,1)} fusion(bf16[2048,256]{1,0:T(8,128)(2,1)S(1)} %bitcast.91, bf16[256,256]{1,0:T(8,128)(2,1)S(1)} %copy-done), kind=kOutput, calls=%fused_computation.25 | convolution fusion | flops 268959744 | bytes 2228224 | tf_op jit(solution)/shard_map/dot_general | solution.py:42
  66.0 1.5 %copy.36 = bf16[2048,256]{0,1:T(8,128)(2,1)S(1)} copy(bf16[2048,256]{1,0:T(8,128)(2,1)} %convolution_convert_fusion) | data formatting | bytes 2097152 | tf_op jit(solution)/shard_map/convert_element_type | solution.py:43
  67.4 0.0 copy-start.5
  67.5 0.0 copy-start.6
  67.5 3.2 %reshape_reshape.11 = bf16[32,64,8,32]{1,0,3,2:T(8,128)(2,1)} reshape(bf16[2048,256]{0,1:T(8,128)(2,1)S(1)} %copy.36) | data formatting | bytes 2097152 | tf_op jit(solution)/shard_map/reshape;reshape | solution.py:28
  70.7 0.0 copy-done.5
  70.7 0.4 convolution_convert_fusion.1
  71.1 0.0 copy-done.6
  71.1 1.4 %convolution_convert_fusion.2 = bf16[2048,256]{1,0:T(8,128)(2,1)} fusion(bf16[2048,256]{1,0:T(8,128)(2,1)S(1)} %bitcast.93, bf16[256,256]{1,0:T(8,128)(2,1)S(1)} %copy-done.6), kind=kOutput, calls=%fused_computation.27 | convolution fusion | flops 268959744 | bytes 2228224 | tf_op jit(solution)/shard_map/dot_general | solution.py:42
  72.5 2.3 %copy.34 = bf16[2048,256]{0,1:T(8,128)(2,1)} copy(bf16[2048,256]{1,0:T(8,128)(2,1)} %convolution_convert_fusion.2) | data formatting | bytes 2097152 | tf_op jit(solution)/shard_map/convert_element_type | solution.py:43
  74.8 0.6 copy.35
  75.4 3.2 %reshape_reshape.10 = bf16[32,64,8,32]{1,0,3,2:T(8,128)(2,1)} reshape(bf16[2048,256]{0,1:T(8,128)(2,1)S(1)} %copy.35) | data formatting | bytes 2097152 | tf_op jit(solution)/shard_map/reshape;reshape | solution.py:27
  78.6 4.6 %reshape_reshape.9 = bf16[32,64,8,32]{1,0,3,2:T(8,128)(2,1)} reshape(bf16[2048,256]{0,1:T(8,128)(2,1)} %copy.34) | data formatting | bytes 2097152 | tf_op jit(solution)/shard_map/reshape;reshape | solution.py:29
  83.2 4.4 %fusion.31 = f32[32,8,64,64]{2,3,1,0:T(8,128)S(1)} fusion(bf16[32,64,8,32]{1,0,3,2:T(8,128)(2,1)S(1)} %copy-done.1, bf16[32,64,8,32]{1,0,3,2:T(8,128)(2,1)} %reshape_reshape.10), kind=kOutput, calls=%fused_computation.42 | convolution fusion | flops 67108864 | bytes 6291456 | tf_op jit(solution)/shard_map/pqhd,pkhd->phqk/dot_general | solution.py:30
  87.5 12.2 %fusion.69 = (f32[32,8,64]{2,1,0:T(8,128)S(1)}, f32[32,8,64,64]{2,3,1,0:T(8,128)S(1)}) fusion(f32[32,8,64,64]{2,3,1,0:T(8,128)S(1)} %fusion.31), kind=kOutput, calls=%fused_computation.87 | output fusion | flops 4194367 | bytes 8454144 | tf_op jit(solution)/shard_map/sub | solution.py:34
  99.7 3.8 %fusion.34 = bf16[32,8,32,64]{3,2,1,0:T(8,128)(2,1)} fusion(f32[32,8,64,64]{2,3,1,0:T(8,128)S(1)} %get-tuple-element.8, f32[32,8,64]{2,1,0:T(8,128)S(1)} %get-tuple-element.7, bf16[32,64,8,32]{1,0,3,2:T(8,128)(2,1)S(1)} %copy-done.3), kind=kOutput, calls=%fused_computation.45 | convolution fusion | flops 69730304 | bytes 6356992 | tf_op jit(solution)/shard_map/phqk,pkhd->pqhd/dot_general | solution.py:36
  103.5 2.7 %copy.41 = bf16[1,32,64,256]{3,1,0,2:T(8,128)(2,1)S(1)} copy(bf16[1,32,64,256]{2,3,1,0:T(8,128)(2,1)} %bitcast.97) | data formatting | bytes 2097152 | tf_op jit(solution)/shard_map/reshape | solution.py:37
  106.2 18.5 %all_to_all.31 = bf16[1,32,64,256]{3,1,0,2:T(8,128)(2,1)S(1)} all-to-all(bf16[1,32,64,256]{3,1,0,2:T(8,128)(2,1)S(1)} %copy.41), channel_id=1, replica_groups=mesh['lat'=32,'lead'=8] {'lead'}, dimensions={2} | all-to-all | bytes 2097152 | tf_op jit(solution)/shard_map/all_to_all | solution.py:63
  124.7 0.6 copy.54
  125.3 0.1 copy.43
  125.4 0.2 copy-done.7
  125.6 1.4 %fusion.37 = bf16[1,256,8,256]{3,2,1,0:T(8,128)(2,1)} fusion(bf16[2048,256]{1,0:T(8,128)(2,1)S(1)} %bitcast.94, bf16[256,256]{1,0:T(8,128)(2,1)S(1)} %copy-done.7, bf16[2048,256]{1,0:T(8,128)(2,1)S(1)} %get-tuple-element.6), kind=kOutput, calls=%fused_computation.46 | convolution fusion | flops 270008320 | bytes 3276800 | tf_op jit(solution)/shard_map/dot_general | solution.py:64
  (9 shorter events, 0.0 us)
Async XLA Ops:
  0.0 64.5 %copy-start = (bf16[256,256]{1,0:T(8,128)(2,1)S(1)}, bf16[256,256]{1,0:T(8,128)(2,1)}, u32[]{:S(2)}) copy-start(bf16[256,256]{1,0:T(8,128)(2,1)} %param.13) | copy-start | bytes 393220
  0.0 37.0 %copy-start.2 = (bf16[1,256,8,256]{3,2,1,0:T(8,128)(2,1)S(1)}, bf16[1,256,8,256]{3,2,1,0:T(8,128)(2,1)}, u32[]{:S(2)}) copy-start(bf16[1,256,8,256]{3,2,1,0:T(8,128)(2,1)} %param.8) | copy-start | bytes 3145732
  0.0 30.9 %collective-permute-start.1 = (bf16[1,256,8,256]{3,2,1,0:T(8,128)(2,1)}, bf16[1,256,8,256]{3,2,1,0:T(8,128)(2,1)S(1)}, u32[]{:S(2)}, u32[]{:S(2)}) collective-permute-start(bf16[1,256,8,256]{3,2,1,0:T(8,128)(2,1)} %param.8), channel_id=1, source_target_pairs={{8,0},{16,8},{24,16},{32,24},{40,32},{48,40},{56,48},{64,56},{72,6... | collective-permute-start | bytes 3145736 | tf_op jit(solution)/shard_map/ppermute | solution.py:18
  8.2 28.8 %collective-permute-start = (bf16[1,256,8,256]{3,2,1,0:T(8,128)(2,1)}, bf16[1,256,8,256]{3,2,1,0:T(8,128)(2,1)S(1)}, u32[]{:S(2)}, u32[]{:S(2)}) collective-permute-start(bf16[1,256,8,256]{3,2,1,0:T(8,128)(2,1)} %param.8), channel_id=1, source_target_pairs={{0,8},{8,16},{16,24},{24,32},{32,40},{40,48},{48,56},{56,64},{64,7... | collective-permute-start | bytes 3145736 | tf_op jit(solution)/shard_map/ppermute | solution.py:15
  11.8 25.8 %copy-start.4 = (bf16[3,3,256,256]{3,2,1,0:T(8,128)(2,1)S(1)}, bf16[3,3,256,256]{3,2,1,0:T(8,128)(2,1)}, u32[]{:S(2)}) copy-start(bf16[3,3,256,256]{3,2,1,0:T(8,128)(2,1)} %param.9) | copy-start | bytes 3538948
  40.2 0.7 copy-start.8
  40.9 2.4 %copy-start.9 = (f32[256]{0:T(256)S(1)}, f32[256]{0:T(256)}, u32[]{:S(2)}) copy-start(f32[256]{0:T(256)} %param.11) | copy-start | bytes 3076
  67.4 3.2 %copy-start.5 = (bf16[256,256]{1,0:T(8,128)(2,1)S(1)}, bf16[256,256]{1,0:T(8,128)(2,1)}, u32[]{:S(2)}) copy-start(bf16[256,256]{1,0:T(8,128)(2,1)} %param.12) | copy-start | bytes 393220
  67.5 3.7 %copy-start.6 = (bf16[256,256]{1,0:T(8,128)(2,1)S(1)}, bf16[256,256]{1,0:T(8,128)(2,1)}, u32[]{:S(2)}) copy-start(bf16[256,256]{1,0:T(8,128)(2,1)} %param.14) | copy-start | bytes 393220
  78.6 4.6 %copy-start.1 = (bf16[32,64,8,32]{1,0,3,2:T(8,128)(2,1)S(1)}, bf16[32,64,8,32]{1,0,3,2:T(8,128)(2,1)}, u32[]{:S(2)}) copy-start(bf16[32,64,8,32]{1,0,3,2:T(8,128)(2,1)} %reshape_reshape.11) | copy-start | bytes 3145732
  87.5 12.2 %copy-start.3 = (bf16[32,64,8,32]{1,0,3,2:T(8,128)(2,1)S(1)}, bf16[32,64,8,32]{1,0,3,2:T(8,128)(2,1)}, u32[]{:S(2)}) copy-start(bf16[32,64,8,32]{1,0,3,2:T(8,128)(2,1)} %reshape_reshape.9) | copy-start | bytes 3145732
  124.7 0.9 copy-start.7
where the time goes:
time: 127 us
  blocking collectives  38.9 us (31%)
  waiting for transfers between devices  25.2 us (20%)
  local copies, waits for them, and re-layouts  19.3 us (15%)
  matrix products  19.2 us (15%)
  other arithmetic  14.1 us (11%)
  starting transfers between devices  10.1 us (8%)
    all_to_all x1, blocking collectives, shards(): lax.all_to_all(normed, 'lead', split_axis=1, concat_axis=2, tiled=True)  20.4 us
    ppermute x1, waiting for transfers between devices, padded_2(): lax.ppermute(lax.slice_in_dim(block, 0, width, axis=dim), axis, backward)  19.1 us
    all_to_all x1, blocking collectives, shards(): lax.all_to_all(attended_px, 'lead', split_axis=2, concat_axis=1, tiled=True)  18.5 us
    sub x1, other arithmetic, attend(): expo = jnp.exp(scores - top)  12.2 us
    ppermute x1, starting transfers between devices, padded_2(): lax.ppermute(lax.slice_in_dim(block, 0, width, axis=dim), axis, backward)  8.15 us
    dot_general x9, matrix products, shards(): jnp.dot(piece, conv_weight[a, b], preferred_element_type=jnp.float32)  6.44 us
    ppermute x1, waiting for transfers between devices, padded_2(): lax.ppermute(lax.slice_in_dim(block, block.shape[dim] - width, None, axis...  6.12 us
    another operation x1, local copies, waits for them, and re-layouts, attend(): values = values.reshape(-1, values.shape[-2], heads, HD)  4.55 us
  transfers between devices with their start and end apart: 2, of which 2 were waited for; matrix products, arithmetic and copies ran while one was open for 1% of the time, Pallas kernels for 0%

commit v1 on v0

--- a/solution.py
+++ b/solution.py
@@ -60,7 +60,12 @@
     normed = normed.reshape(nrows, width, leads, chans)
     block = lax.all_to_all(normed, "lead", split_axis=1, concat_axis=2, tiled=True)
     attended_px = attend(project(block, w_query), project(block, w_key), project(block, w_value))
-    attended = lax.all_to_all(attended_px, "lead", split_axis=2, concat_axis=1, tiled=True)
+    attended = jnp.concatenate(
+        lax.all_to_all(
+            jnp.stack(jnp.split(attended_px, lax.axis_size("lead"), axis=2)), "lead", 0, 0
+        ),
+        axis=1,
+    )
     mixed = hidden_f + jnp.dot(
         attended.reshape(-1, chans), w_out, preferred_element_type=jnp.float32
     )

time: 127 us -> 152 us (1.20)
  local copies, waits for them, and re-layouts: 19.3 us -> 44.9 us
    unnamed x20 -> x37, local copies, waits for them, and re-layouts: 0.53 us -> 21.8 us
    split x0 -> x1, local copies, waits for them, and re-layouts: none -> 7.66 us  [shards(): jnp.split(attended_px, lax.axis_size('lead'), axis=2)]
    reshape x1 -> x0, local copies, waits for them, and re-layouts: 2.68 us -> none  [attend(): return attended.astype(jnp.bfloat16).reshape(q_shape)]
where the time goes in v1:
time: 152 us; the launch traced here: 151 us
  local copies, waits for them, and re-layouts  44.9 us (30%)
  blocking collectives  39 us (26%)
  waiting for transfers between devices  25.2 us (17%)
  matrix products  17.9 us (12%)
  other arithmetic  14.1 us (9%)
  starting transfers between devices  10.1 us (7%)
    unnamed x37, local copies, waits for them, and re-layouts  21.8 us
    all_to_all x1, blocking collectives, shards(): lax.all_to_all(normed, 'lead', split_axis=1, concat_axis=2, tiled=True)  20.4 us
    ppermute x1, waiting for transfers between devices, padded_2(): lax.ppermute(lax.slice_in_dim(block, 0, width, axis=dim), axis, backward)  19.1 us
    all_to_all x1, blocking collectives, shards(): lax.all_to_all(jnp.stack(jnp.split(attended_px, lax.axis_size('lead'), ax...  18.7 us
    sub x1, other arithmetic, attend(): expo = jnp.exp(scores - top)  12.2 us
    ppermute x1, starting transfers between devices, padded_2(): lax.ppermute(lax.slice_in_dim(block, 0, width, axis=dim), axis, backward)  8.15 us
    split x1, local copies, waits for them, and re-layouts, shards(): jnp.split(attended_px, lax.axis_size('lead'), axis=2)  7.66 us
    dot_general x9, matrix products, shards(): jnp.dot(piece, conv_weight[a, b], preferred_element_type=jnp.float32)  6.44 us
  transfers between devices with their start and end apart: 2, of which 2 were waited for; matrix products, arithmetic and copies ran while one was open for 1% of the time, Pallas kernels for 0%

profile of v1, /device:TPU:6, one launch (start us, length us, event | category | flops | bytes accessed | tf_op | source)
XLA Modules:
  0.0 151.5 jit_solution(10507997193463628305)
XLA Ops:
  0.0 8.1 %collective-permute-start.1 = (bf16[1,256,8,256]{3,2,1,0:T(8,128)(2,1)}, bf16[1,256,8,256]{3,2,1,0:T(8,128)(2,1)S(1)}, u32[]{:S(2)}, u32[]{:S(2)}) collective-permute-start(bf16[1,256,8,256]{3,2,1,0:T(8,128)(2,1)} %param.8), channel_id=1, source_target_pairs={{8,0},{16,8},{24,16},{32,24},{40,32},{48,40},{56,48},{64,56},{72,6... | collective-permute-start | bytes 3145736 | tf_op jit(solution)/shard_map/ppermute | solution.py:18
  8.2 1.9 %collective-permute-start = (bf16[1,256,8,256]{3,2,1,0:T(8,128)(2,1)}, bf16[1,256,8,256]{3,2,1,0:T(8,128)(2,1)S(1)}, u32[]{:S(2)}, u32[]{:S(2)}) collective-permute-start(bf16[1,256,8,256]{3,2,1,0:T(8,128)(2,1)} %param.8), channel_id=1, source_target_pairs={{0,8},{8,16},{16,24},{24,32},{32,40},{40,48},{48,56},{56,64},{64,7... | collective-permute-start | bytes 3145736 | tf_op jit(solution)/shard_map/ppermute | solution.py:15
  10.1 1.7 %fusion.46 = f32[2048,256]{1,0:T(8,128)S(1)} fusion(bf16[1,256,8,256]{3,2,1,0:T(8,128)(2,1)} %param.8, bf16[3,3,256,256]{3,2,1,0:T(8,128)(2,1)} %param.9), kind=kOutput, calls=%fused_computation.61 | convolution fusion | flops 268435456 | bytes 3276800 | tf_op jit(solution)/shard_map/dot_general | solution.py:54
  11.8 0.0 copy-start.5
  11.8 19.1 %collective-permute-done.1 = bf16[1,256,8,256]{3,2,1,0:T(8,128)(2,1)S(1)} collective-permute-done((bf16[1,256,8,256]{3,2,1,0:T(8,128)(2,1)}, bf16[1,256,8,256]{3,2,1,0:T(8,128)(2,1)S(1)}, u32[]{:S(2)}, u32[]{:S(2)}) %collective-permute-start.1) | collective-permute-done | bytes 1048608 | tf_op jit(solution)/shard_map/ppermute | solution.py:18
  30.9 6.1 %collective-permute-done = bf16[1,256,8,256]{3,2,1,0:T(8,128)(2,1)S(1)} collective-permute-done((bf16[1,256,8,256]{3,2,1,0:T(8,128)(2,1)}, bf16[1,256,8,256]{3,2,1,0:T(8,128)(2,1)S(1)}, u32[]{:S(2)}, u32[]{:S(2)}) %collective-permute-start) | collective-permute-done | bytes 1048608 | tf_op jit(solution)/shard_map/ppermute | solution.py:15
  37.0 0.6 fusion.11
  37.6 0.4 fusion.40
  38.0 0.4 fusion.41
  38.4 0.4 fusion.42
  38.9 0.4 fusion.43
  39.3 0.4 fusion.39
  39.8 0.4 fusion.48
  40.2 0.4 fusion.44
  40.6 0.2 copy-done.9
  40.9 1.7 %convert_reduce_fusion = (f32[2048]{0:T(1024)S(1)}, bf16[2048,256]{1,0:T(8,128)(2,1)S(1)}) fusion(f32[256]{0:T(256)S(1)} %copy-done.9, f32[2048,256]{1,0:T(8,128)S(1)} %fusion.39, f32[2048,256]{1,0:T(8,128)S(1)} %fusion.44, f32[2048,256]{1,0:T(8,128)S(1)} %fusion.40, bf16[3,3,256,256]{3,2,1,0:T(8,128)(2,1)S(1)} %copy-done.5, ...), kind=kOutput, calls=%fused_computation.17 | convolution fusion | flops 278919168 | bytes 19014656 | tf_op jit(solution)/shard_map/dot_general | solution.py:54
  42.6 0.6 fusion.19
  43.3 0.7 fusion.38
  44.0 20.4 %all_to_all.20 = bf16[1,256,8,256]{3,2,0,1:T(8,128)(2,1)S(1)} all-to-all(bf16[1,256,8,256]{3,2,0,1:T(8,128)(2,1)S(1)} %fusion.38), channel_id=1, replica_groups=mesh['lat'=32,'lead'=8] {'lead'}, dimensions={1} | all-to-all | bytes 2097152 | tf_op jit(solution)/shard_map/all_to_all | solution.py:61
  64.4 0.1 copy.45
  64.6 1.4 convolution_convert_fusion
  66.0 1.5 copy.48
  67.5 3.2 %reshape_reshape.14 = bf16[32,64,8,32]{1,0,3,2:T(8,128)(2,1)} reshape(bf16[2048,256]{0,1:T(8,128)(2,1)S(1)} %copy.48) | data formatting | bytes 2097152 | tf_op jit(solution)/shard_map/reshape;reshape | solution.py:28
  70.7 0.4 convolution_convert_fusion.1
  71.1 1.4 convolution_convert_fusion.2
  72.5 2.3 %copy.46 = bf16[2048,256]{0,1:T(8,128)(2,1)} copy(bf16[2048,256]{1,0:T(8,128)(2,1)} %convolution_convert_fusion.2) | data formatting | bytes 2097152 | tf_op jit(solution)/shard_map/convert_element_type | solution.py:43
  74.8 0.6 copy.47
  75.4 3.2 %reshape_reshape.13 = bf16[32,64,8,32]{1,0,3,2:T(8,128)(2,1)} reshape(bf16[2048,256]{0,1:T(8,128)(2,1)S(1)} %copy.47) | data formatting | bytes 2097152 | tf_op jit(solution)/shard_map/reshape;reshape | solution.py:27
  78.6 4.6 %reshape_reshape.12 = bf16[32,64,8,32]{1,0,3,2:T(8,128)(2,1)} reshape(bf16[2048,256]{0,1:T(8,128)(2,1)} %copy.46) | data formatting | bytes 2097152 | tf_op jit(solution)/shard_map/reshape;reshape | solution.py:29
  83.2 4.4 %fusion.31 = f32[32,8,64,64]{2,3,1,0:T(8,128)S(1)} fusion(bf16[32,64,8,32]{1,0,3,2:T(8,128)(2,1)S(1)} %copy-done.2, bf16[32,64,8,32]{1,0,3,2:T(8,128)(2,1)} %reshape_reshape.13), kind=kOutput, calls=%fused_computation.42 | convolution fusion | flops 67108864 | bytes 6291456 | tf_op jit(solution)/shard_map/pqhd,pkhd->phqk/dot_general | solution.py:30
  87.5 12.2 %fusion.70 = (f32[32,8,64]{2,1,0:T(8,128)S(1)}, f32[32,8,64,64]{2,3,1,0:T(8,128)S(1)}) fusion(f32[32,8,64,64]{2,3,1,0:T(8,128)S(1)} %fusion.31), kind=kOutput, calls=%fused_computation.95 | output fusion | flops 4194367 | bytes 8454144 | tf_op jit(solution)/shard_map/sub | solution.py:34
  99.7 2.5 %fusion.34 = bf16[32,8,32,64]{3,2,1,0:T(8,128)(2,1)S(1)} fusion(f32[32,8,64,64]{2,3,1,0:T(8,128)S(1)} %get-tuple-element.16, f32[32,8,64]{2,1,0:T(8,128)S(1)} %get-tuple-element.15, bf16[32,64,8,32]{1,0,3,2:T(8,128)(2,1)S(1)} %copy-done.4), kind=kOutput, calls=%fused_computation.45 | convolution fusion | flops 69730304 | bytes 6356992 | tf_op jit(solution)/shard_map/phqk,pkhd->pqhd/dot_general | solution.py:36
  102.2 7.7 %fusion.69 = (bf16[1,32,8,256]{2,3,1,0:T(8,128)(2,1)}, bf16[1,32,8,256]{2,3,1,0:T(8,128)(2,1)}, bf16[1,32,8,256]{2,3,1,0:T(8,128)(2,1)}, bf16[1,32,8,256]{2,3,1,...) fusion(bf16[1,32,64,256]{2,3,1,0:T(8,128)(2,1)S(1)} %bitcast.102), kind=kLoop, calls=%fused_computation.94 | loop fusion | bytes 2097152 | tf_op jit(solution)/shard_map/split | solution.py:65
  109.9 1.8 %copy.69 = bf16[1,32,8,256]{3,2,1,0:T(8,128)(2,1)S(1)} copy(bf16[1,32,8,256]{2,3,1,0:T(8,128)(2,1)} %get-tuple-element.5) | data formatting | bytes 262144
  111.7 1.9 %copy.68 = bf16[1,32,8,256]{3,2,1,0:T(8,128)(2,1)S(1)} copy(bf16[1,32,8,256]{2,3,1,0:T(8,128)(2,1)} %get-tuple-element.6) | data formatting | bytes 262144
  113.6 1.9 %copy.67 = bf16[1,32,8,256]{3,2,1,0:T(8,128)(2,1)S(1)} copy(bf16[1,32,8,256]{2,3,1,0:T(8,128)(2,1)} %get-tuple-element.7) | data formatting | bytes 262144
  115.4 2.5 %copy.66 = bf16[1,32,8,256]{3,2,1,0:T(8,128)(2,1)} copy(bf16[1,32,8,256]{2,3,1,0:T(8,128)(2,1)} %get-tuple-element.8) | data formatting | bytes 262144
  117.9 2.5 %copy.65 = bf16[1,32,8,256]{3,2,1,0:T(8,128)(2,1)} copy(bf16[1,32,8,256]{2,3,1,0:T(8,128)(2,1)} %get-tuple-element.9) | data formatting | bytes 262144
  120.4 2.5 %copy.64 = bf16[1,32,8,256]{3,2,1,0:T(8,128)(2,1)} copy(bf16[1,32,8,256]{2,3,1,0:T(8,128)(2,1)} %get-tuple-element.10) | data formatting | bytes 262144
  122.8 2.5 %copy.63 = bf16[1,32,8,256]{3,2,1,0:T(8,128)(2,1)} copy(bf16[1,32,8,256]{2,3,1,0:T(8,128)(2,1)} %get-tuple-element.11) | data formatting | bytes 262144
  125.3 1.4 copy.62
  126.7 0.9 bitcast_dynamic-update-slice_fusion.7
  127.7 0.9 bitcast_dynamic-update-slice_fusion.6
  128.6 0.9 bitcast_dynamic-update-slice_fusion.5
  129.5 0.9 bitcast_dynamic-update-slice_fusion.4
  130.4 0.9 bitcast_dynamic-update-slice_fusion.3
  131.4 18.7 %all_to_all.21 = bf16[8,1,32,8,256]{4,3,2,1,0:T(8,128)(2,1)S(1)} all-to-all(bf16[8,1,32,8,256]{4,3,2,1,0:T(8,128)(2,1)S(1)} %bitcast_dynamic-update-slice_fusion), channel_id=1, replica_groups=mesh['lat'=32,'lead'=8] {'lead'}, dimensions={0} | all-to-all | bytes 2097152 | tf_op jit(solution)/shard_map/all_to_all | solution.py:64
  150.1 1.4 fusion.37
  (25 shorter events, 0.1 us)
Async XLA Ops:
  0.0 64.5 %copy-start = (bf16[256,256]{1,0:T(8,128)(2,1)S(1)}, bf16[256,256]{1,0:T(8,128)(2,1)}, u32[]{:S(2)}) copy-start(bf16[256,256]{1,0:T(8,128)(2,1)} %param.13) | copy-start | bytes 393220
  0.0 37.0 %copy-start.3 = (bf16[1,256,8,256]{3,2,1,0:T(8,128)(2,1)S(1)}, bf16[1,256,8,256]{3,2,1,0:T(8,128)(2,1)}, u32[]{:S(2)}) copy-start(bf16[1,256,8,256]{3,2,1,0:T(8,128)(2,1)} %param.8) | copy-start | bytes 3145732
  0.0 30.9 %collective-permute-start.1 = (bf16[1,256,8,256]{3,2,1,0:T(8,128)(2,1)}, bf16[1,256,8,256]{3,2,1,0:T(8,128)(2,1)S(1)}, u32[]{:S(2)}, u32[]{:S(2)}) collective-permute-start(bf16[1,256,8,256]{3,2,1,0:T(8,128)(2,1)} %param.8), channel_id=1, source_target_pairs={{8,0},{16,8},{24,16},{32,24},{40,32},{48,40},{56,48},{64,56},{72,6... | collective-permute-start | bytes 3145736 | tf_op jit(solution)/shard_map/ppermute | solution.py:18
  8.2 28.8 %collective-permute-start = (bf16[1,256,8,256]{3,2,1,0:T(8,128)(2,1)}, bf16[1,256,8,256]{3,2,1,0:T(8,128)(2,1)S(1)}, u32[]{:S(2)}, u32[]{:S(2)}) collective-permute-start(bf16[1,256,8,256]{3,2,1,0:T(8,128)(2,1)} %param.8), channel_id=1, source_target_pairs={{0,8},{8,16},{16,24},{24,32},{32,40},{40,48},{48,56},{56,64},{64,7... | collective-permute-start | bytes 3145736 | tf_op jit(solution)/shard_map/ppermute | solution.py:15
  11.8 25.8 %copy-start.5 = (bf16[3,3,256,256]{3,2,1,0:T(8,128)(2,1)S(1)}, bf16[3,3,256,256]{3,2,1,0:T(8,128)(2,1)}, u32[]{:S(2)}) copy-start(bf16[3,3,256,256]{3,2,1,0:T(8,128)(2,1)} %param.9) | copy-start | bytes 3538948
  40.2 0.7 copy-start.9
  40.9 2.4 %copy-start.10 = (f32[256]{0:T(256)S(1)}, f32[256]{0:T(256)}, u32[]{:S(2)}) copy-start(f32[256]{0:T(256)} %param.11) | copy-start | bytes 3076
  67.4 3.2 %copy-start.6 = (bf16[256,256]{1,0:T(8,128)(2,1)S(1)}, bf16[256,256]{1,0:T(8,128)(2,1)}, u32[]{:S(2)}) copy-start(bf16[256,256]{1,0:T(8,128)(2,1)} %param.12) | copy-start | bytes 393220
  67.5 3.6 %copy-start.7 = (bf16[256,256]{1,0:T(8,128)(2,1)S(1)}, bf16[256,256]{1,0:T(8,128)(2,1)}, u32[]{:S(2)}) copy-start(bf16[256,256]{1,0:T(8,128)(2,1)} %param.14) | copy-start | bytes 393220
  78.6 4.6 %copy-start.2 = (bf16[32,64,8,32]{1,0,3,2:T(8,128)(2,1)S(1)}, bf16[32,64,8,32]{1,0,3,2:T(8,128)(2,1)}, u32[]{:S(2)}) copy-start(bf16[32,64,8,32]{1,0,3,2:T(8,128)(2,1)} %reshape_reshape.14) | copy-start | bytes 3145732
  87.5 12.2 %copy-start.4 = (bf16[32,64,8,32]{1,0,3,2:T(8,128)(2,1)S(1)}, bf16[32,64,8,32]{1,0,3,2:T(8,128)(2,1)}, u32[]{:S(2)}) copy-start(bf16[32,64,8,32]{1,0,3,2:T(8,128)(2,1)} %reshape_reshape.12) | copy-start | bytes 3145732
  126.7 23.3 %copy-start.8 = (bf16[256,256]{1,0:T(8,128)(2,1)S(1)}, bf16[256,256]{1,0:T(8,128)(2,1)}, u32[]{:S(2)}) copy-start(bf16[256,256]{1,0:T(8,128)(2,1)} %param.15) | copy-start | bytes 393220
  131.4 20.1 %copy-start.1 = (bf16[256,256]{1,0:T(8,128)(2,1)S(1)}, bf16[256,256]{1,0:T(8,128)(2,1)}, u32[]{:S(2)}) copy-start(bf16[256,256]{1,0:T(8,128)(2,1)} %param.13) | copy-start | bytes 393220
